TPU v7x, 256 devices: a whole 4x4x8 slice. The times are simulated.
256 devices in a mesh: req: 4 (over y), vocab: 64 (over z, x, core).
Axes of the slice: x: 4, y: 4, z: 8, core: 2. Of those that a mesh axis runs over, the one named last changes fastest.
Arguments:
- hidden: bfloat16 [8192, 4096], P('req', 'vocab'), may hold values from -320 to 320
- gain: float32 [4096], replicated, may hold values from 0.5 to 1.5
- head: bfloat16 [4096, 32768], P(None, ('req', 'vocab'))
- targets: int32 [8192], P('req'), may hold values from 0 to 32767
- lengths: int32 [4, 4], P('req'), may hold values from 1 to 1280, 2048 in all within a row
Outputs:
- token_logprob: float32 [8192], P(('req', 'vocab'))
- token_entropy: float32 [8192], P(('req', 'vocab'))
- seq_logprob: float32 [12], P('req')
- seq_entropy: float32 [12], P('req')
Inputs may be any that keep to these rules, and one draw needn't show every extreme that they name: lengths[q, 3] counts the empty slots at the end of index q's rows.
All inputs are finite; a program needn't handle non-finite values.
Results may differ from a plain program's by a relative error of at most 0.0012.
Values may be sent and summed in bfloat16 or wider, within the bound.
A program may use at most 128 MiB of HBM per device.

v0:
```python
import jax
import jax.numpy as jnp
from jax import lax
from jax.sharding import Mesh
from jax.sharding import PartitionSpec as P

D = 4096
SEQ_DEV = 3
VOCAB = ("vocab_0", "vocab_1", "vocab_2")
REQ_VOCAB = ("req", "vocab_0", "vocab_1", "vocab_2")
EPS = 1e-05


def gathered_once(shard, axis):
    leaves = jax.tree.leaves(shard)
    order = sorted(range(len(leaves)), key=lambda k: -leaves[k].size)
    width = (1, *leaves[order[0]].shape)[-1]
    lines = [
        jnp.pad(leaves[k].reshape(-1), (0, -leaves[k].size % width)).reshape(-1, width)
        for k in order
    ]
    both, at, found = (lax.all_gather(jnp.concatenate(lines), axis), 0, {})
    for k, line in zip(order, lines):
        slab = both[:, at : at + len(line)].reshape(len(both), -1)
        found[k] = slab[:, : leaves[k].size].reshape(-1, *leaves[k].shape)
        at += len(line)
    numbers = iter(range(len(leaves)))
    return jax.tree.map(lambda _: found[next(numbers)], shard)


def combined_by_axis(shard, axes, combine):
    for axis in axes:
        pieces = gathered_once(shard, axis)
        shard = jax.tree.map(lambda part: part[0], pieces)
        for k in range(1, lax.axis_size(axis)):
            shard = combine(shard, jax.tree.map(lambda part: part[k], pieces))
    return shard


def combine_stats(first, second):
    peak = jnp.maximum(first[0], second[0])
    scale_first = jnp.exp(first[0] - peak)
    scale_second = jnp.exp(second[0] - peak)
    return (
        peak,
        first[1] * scale_first + second[1] * scale_second,
        first[2] * scale_first + second[2] * scale_second,
        first[3] + second[3],
    )


def finish_rows(peak, total, moment, picked):
    log_total = peak + jnp.log(total)
    return (picked - log_total, log_total - moment / total)


def shards(hidden, gain, head, targets, lengths):
    rows = hidden.shape[0]
    vocab_index = lax.axis_index(VOCAB)
    vocab_count = lax.axis_size(VOCAB)
    shard_cols = head.shape[1]
    width_cols = shard_cols * lax.axis_size("req")
    col_pos = jnp.arange(width_cols, dtype=jnp.int32)
    col_ids = (
        col_pos // shard_cols * (vocab_count * shard_cols)
        + vocab_index * shard_cols
        + col_pos % shard_cols
    )
    block = min(512, rows)
    count = rows // block
    seq_lens = lengths[0, :SEQ_DEV]
    ends = jnp.cumsum(seq_lens)
    starts = ends - seq_lens
    live = ends[-1]
    full_rows = lax.all_gather(hidden, VOCAB, axis=1, tiled=True)
    values = full_rows.astype(jnp.float32)
    mean_sq = jnp.sum(values * values, axis=1) / D
    normed = (values * lax.rsqrt(mean_sq + EPS)[:, None] * gain[None, :]).astype(jnp.bfloat16)
    columns = lax.all_gather(head, "req", axis=1, tiled=True)

    def block_logits(start):
        rows_blk = lax.dynamic_slice_in_dim(normed, start, block, 0)
        return jnp.dot(rows_blk, columns, preferred_element_type=jnp.float32)

    def compute_block(start):
        logits = block_logits(start)
        wanted = lax.dynamic_slice_in_dim(targets, start, block, 0)
        peak = jnp.max(logits, axis=1)
        weights = jnp.exp(logits - peak[:, None])
        total = jnp.sum(weights, axis=1)
        moment = jnp.sum(weights * logits, axis=1)
        picked = jnp.sum(jnp.where(col_ids[None, :] == wanted[:, None], logits, 0.0), axis=1)
        return (peak, total, moment, picked)

    def one_block(block_index):
        start = block_index * block
        return compute_block(start)

    peak, total, moment, picked = lax.map(one_block, jnp.arange(count, dtype=jnp.int32))
    peak = peak.reshape(rows)
    total = total.reshape(rows)
    moment = moment.reshape(rows)
    picked = picked.reshape(rows)
    share = rows // vocab_count
    divisor = seq_lens.astype(jnp.float32)
    peak, total, moment, picked = combined_by_axis(
        (peak, total, moment, picked), VOCAB, combine_stats
    )
    logprob, entropy = finish_rows(peak, total, moment, picked)
    local = jnp.arange(rows, dtype=jnp.int32)
    valid = local < live
    logprob = jnp.where(valid, logprob, 0.0)
    entropy = jnp.where(valid, entropy, 0.0)
    member = ((local[None, :] >= starts[:, None]) & (local[None, :] < ends[:, None])).astype(
        jnp.float32
    )
    seq_lp = jnp.sum(member * logprob[None, :], axis=1) / divisor
    seq_ent = jnp.sum(member * entropy[None, :], axis=1) / divisor
    own_lp = lax.dynamic_slice_in_dim(logprob, vocab_index * share, share, 0)
    own_ent = lax.dynamic_slice_in_dim(entropy, vocab_index * share, share, 0)
    return (own_lp, own_ent, seq_lp, seq_ent)


def solution(mesh):
    split = Mesh(
        mesh.devices.reshape(mesh.shape["req"], 8, 4, 2), ("req", "vocab_0", "vocab_1", "vocab_2")
    )
    placed = (P("req", VOCAB), P(), P(None, REQ_VOCAB), P("req"), P("req", None))
    return jax.shard_map(
        shards,
        mesh=split,
        in_specs=placed,
        out_specs=(P(REQ_VOCAB), P(REQ_VOCAB), P("req"), P("req")),
        check_vma=False,
    )
```

profile of v0, /device:TPU:1, one launch (start us, length us, event | category | flops | bytes accessed | tf_op | source)
XLA Modules:
  0.0 251.6 jit_solution(500161678944132281)
XLA Ops:
  7.2 0.7 all-gather.9.cloned.1.call-update
  8.0 0.7 all-gather.11.cloned.1.call-update
  8.7 0.7 slice_bitcast_fusion.36
  10.1 0.7 bitcast_subtract_fusion
  10.8 103.4 %all-gather.9.cloned.1.call-done = bf16[2048,4096]{0,1:T(8,128)(2,1)} async-done(((bf16[2048,64]{0,1:T(8,128)(2,1)}), bf16[2048,4096]{0,1:T(8,128)(2,1)}) %all-gather.9.cloned.1.call-update) | async-done | bytes 16777232 | tf_op jit(solution)/shard_map/all_gather | solution.py:75
  114.2 7.7 %fusion.16 = f32[2048]{0:T(1024)S(1)} fusion(bf16[2048,4096]{0,1:T(8,128)(2,1)} %all-gather.9.cloned.1.call-done), kind=kLoop, calls=%fused_computation.24 | loop fusion | flops 25163776 | bytes 16785408 | tf_op jit(solution)/shard_map/reduce_sum | solution.py:77
  121.9 3.4 %copy-done = bf16[2048,4096]{0,1:T(8,128)(2,1)S(1)} copy-done((bf16[2048,4096]{0,1:T(8,128)(2,1)S(1)}, bf16[2048,4096]{0,1:T(8,128)(2,1)}, u32[]{:S(2)}) %copy-start) | copy-done | bytes 16777240
  125.3 8.7 %fusion.18 = bf16[2048,4096]{0,1:T(8,128)(2,1)} fusion(bf16[2048,4096]{0,1:T(8,128)(2,1)S(1)} %copy-done, f32[4096]{0:T(1024)S(1)} %copy-done.1, f32[2048]{0:T(1024)S(1)} %add_rsqrt_fusion), kind=kLoop, calls=%fused_computation.26 | loop fusion | flops 33554432 | bytes 33579008 | tf_op jit(solution)/shard_map/convert_element_type | solution.py:78
  134.0 31.2 %all-gather.11.cloned.1.call-done = bf16[4096,512]{1,0:T(8,128)(2,1)} async-done(((bf16[4096,128]{1,0:T(8,128)(2,1)}), bf16[4096,512]{1,0:T(8,128)(2,1)}) %all-gather.11.cloned.1.call-update) | async-done | bytes 4194320 | tf_op jit(solution)/shard_map/all_gather | solution.py:79
  165.2 33.8 %while.17 = (s32[]{:T(128)}, f32[4,512]{1,0:T(4,128)S(1)}, f32[4,512]{1,0:T(4,128)S(1)}, f32[4,512]{1,0:T(4,128)S(1)}, f32[4,512]{1,0:T(4,128)S(1)}, /*index=5*/...) while((s32[]{:T(128)}, f32[4,512]{1,0:T(4,128)S(1)}, ...), condition=%wide.region_7.8_spmd.clone, body=%wide.region_2.7_spmd.clone.sunk | while | flops 2149586432 | bytes 10522843 | solution.py:99
  166.5 5.9 %fusion.105 = (f32[512]{0:T(512)S(1)}, f32[512,512]{0,1:T(8,128)S(1)}) fusion(bf16[4096,512]{1,0:T(8,128)(2,1)} %get-tuple-element.256, bf16[2048,4096]{0,1:T(8,128)(2,1)} %get-tuple-element.255, s32[]{:T(128)S(6)} %select_n.72), kind=kOutput, calls=%fused_computation.187.clone.1 | convolution fusion | flops 2147745280 | bytes 9439236 | tf_op jit(solution)/shard_map/while/body/eval_jaxpr/dot_general | solution.py:83
  172.3 0.8 dynamic_slice.30
  173.7 0.6 dynamic_slice.29
  174.9 5.9 %fusion.105 = (f32[512]{0:T(512)S(1)}, f32[512,512]{0,1:T(8,128)S(1)}) fusion(bf16[4096,512]{1,0:T(8,128)(2,1)} %get-tuple-element.256, bf16[2048,4096]{0,1:T(8,128)(2,1)} %get-tuple-element.255, s32[]{:T(128)S(6)} %select_n.72), kind=kOutput, calls=%fused_computation.187.clone.1 | convolution fusion | flops 2147745280 | bytes 9439236 | tf_op jit(solution)/shard_map/while/body/eval_jaxpr/dot_general | solution.py:83
  180.8 0.8 dynamic_slice.30
  183.4 5.9 %fusion.105 = (f32[512]{0:T(512)S(1)}, f32[512,512]{0,1:T(8,128)S(1)}) fusion(bf16[4096,512]{1,0:T(8,128)(2,1)} %get-tuple-element.256, bf16[2048,4096]{0,1:T(8,128)(2,1)} %get-tuple-element.255, s32[]{:T(128)S(6)} %select_n.72), kind=kOutput, calls=%fused_computation.187.clone.1 | convolution fusion | flops 2147745280 | bytes 9439236 | tf_op jit(solution)/shard_map/while/body/eval_jaxpr/dot_general | solution.py:83
  189.2 0.8 dynamic_slice.30
  191.8 5.9 %fusion.105 = (f32[512]{0:T(512)S(1)}, f32[512,512]{0,1:T(8,128)S(1)}) fusion(bf16[4096,512]{1,0:T(8,128)(2,1)} %get-tuple-element.256, bf16[2048,4096]{0,1:T(8,128)(2,1)} %get-tuple-element.255, s32[]{:T(128)S(6)} %select_n.72), kind=kOutput, calls=%fused_computation.187.clone.1 | convolution fusion | flops 2147745280 | bytes 9439236 | tf_op jit(solution)/shard_map/while/body/eval_jaxpr/dot_general | solution.py:83
  197.7 0.8 dynamic_slice.30
  199.1 20.3 %all-gather.3 = f32[8,4,2048]{2,1,0:T(4,128)S(1)} all-gather(f32[1,4,2048]{2,1,0:T(4,128)S(1)} %maximum_bitcast_fusion), channel_id=2, replica_groups=mesh['req'=4,'vocab_0'=8,'vocab_1'=4,'vocab_2'=2] {'vocab_0'}, dimensions={0}, use_global_device_ids=true | all-gather | bytes 294912 | tf_op jit(solution)/shard_map/all_gather | solution.py:22
  219.9 9.4 %all-gather.4 = f32[4,4,2048]{2,1,0:T(4,128)S(1)} all-gather(f32[1,4,2048]{2,1,0:T(4,128)S(1)} %maximum_bitcast_fusion.1), channel_id=3, replica_groups=mesh['req'=4,'vocab_0'=8,'vocab_1'=4,'vocab_2'=2] {'vocab_1'}, dimensions={0}, use_global_device_ids=true | all-gather | bytes 163840 | tf_op jit(solution)/shard_map/all_gather | solution.py:22
  229.6 12.5 %all-gather.5 = f32[2,4,2048]{2,1,0:T(4,128)S(1)} all-gather(f32[1,4,2048]{2,1,0:T(4,128)S(1)} %maximum_bitcast_fusion.2), channel_id=4, replica_groups=mesh['req'=4,'vocab_0'=8,'vocab_1'=4,'vocab_2'=2] {'vocab_2'}, dimensions={0}, use_global_device_ids=true | all-gather | bytes 98304 | tf_op jit(solution)/shard_map/all_gather | solution.py:22
  242.1 0.7 subtract_select_fusion
  242.8 0.6 dynamic_slice.17
  (59 shorter events, 7.0 us)
Async XLA Ops:
  7.2 114.7 %copy-start.1 = (f32[4096]{0:T(1024)S(1)}, f32[4096]{0:T(1024)}, u32[]{:S(2)}) copy-start(f32[4096]{0:T(1024)} %param.8) | copy-start | bytes 49156
  7.2 107.0 %all-gather.9.cloned.1.call-start = ((), (), s32[]{:S(2)}) async-start(), calls=%async_computation | async-start | bytes 17039360 | tf_op jit(solution)/shard_map/all_gather | solution.py:75
  7.9 157.3 %all-gather.11.cloned.1.call-start = ((), (), s32[]{:S(2)}) async-start(), calls=%async_computation.1 | async-start | bytes 5242880 | tf_op jit(solution)/shard_map/all_gather | solution.py:79
  114.2 11.1 %copy-start = (bf16[2048,4096]{0,1:T(8,128)(2,1)S(1)}, bf16[2048,4096]{0,1:T(8,128)(2,1)}, u32[]{:S(2)}) copy-start(bf16[2048,4096]{0,1:T(8,128)(2,1)} %all-gather.9.cloned.1.call-done) | copy-start | bytes 50331652
  165.2 79.0 %copy-start.2 = (s32[1,4]{1,0:T(1,128)S(1)}, s32[1,4]{1,0:T(1,128)}, u32[]{:S(2)}) copy-start(s32[1,4]{1,0:T(1,128)} %param.11) | copy-start | bytes 52
Sparse Core Ops, SparseCore 0:
  10.8 103.3 all-gather.8
  116.0 49.1 all-gather.10
where the time goes:
time: 252 us
  waiting for transfers between devices  136 us (54%)
  blocking collectives  42.2 us (17%)
  matrix products  23.5 us (9%)
  other arithmetic  20.9 us (8%)
  between operations  14.2 us (6%)
  local copies, waits for them, and re-layouts  12.1 us (5%)
  loops' own time  2.75 us (1%)
    all_gather x1, waiting for transfers between devices, shards(): full_rows = lax.all_gather(hidden, VOCAB, axis=1, tiled=True)  103 us
    all_gather x3, blocking collectives, gathered_once(): both, at, found = (lax.all_gather(jnp.concatenate(lines), axis), 0, {})  42.2 us
    all_gather x1, waiting for transfers between devices, shards(): columns = lax.all_gather(head, 'req', axis=1, tiled=True)  31.2 us
    dot_general x4, matrix products, block_logits(): return jnp.dot(rows_blk, columns, preferred_element_type=jnp.float32)  23.5 us
    convert_element_type x1, other arithmetic, shards(): (values * lax.rsqrt(mean_sq + EPS)[:, None] * gain[None, :]).astype(jnp.b...  8.73 us
    reduce_sum x1, other arithmetic, shards(): mean_sq = jnp.sum(values * values, axis=1) / D  7.68 us
  transfers between devices with their start and end apart: 2, of which 2 were waited for; matrix products, arithmetic and copies ran while one was open for 7% of the time, Pallas kernels for 0%

commit v1 on v0

--- a/solution.py
+++ b/solution.py
@@ -76,7 +76,8 @@
     values = full_rows.astype(jnp.float32)
     mean_sq = jnp.sum(values * values, axis=1) / D
     normed = (values * lax.rsqrt(mean_sq + EPS)[:, None] * gain[None, :]).astype(jnp.bfloat16)
-    columns = lax.all_gather(head, "req", axis=1, tiled=True)
+    outgoing = jnp.stack([head] * lax.axis_size("req"))
+    columns = jnp.concatenate(lax.all_to_all(outgoing, "req", 0, 0), axis=1)
 
     def block_logits(start):
         rows_blk = lax.dynamic_slice_in_dim(normed, start, block, 0)

time: 252 us -> 217 us (0.86)
  waiting for transfers between devices: 136 us -> 83.1 us
  local copies, waits for them, and re-layouts: 12.1 us -> 28.6 us
  starting transfers between devices: 0.08 us -> 5.04 us
  blocking collectives: 42.2 us -> 38.6 us
    all_gather x1, waiting for transfers between devices: 103 us -> 37.3 us  [shards(): full_rows = lax.all_gather(hidden, VOCAB, axis=1, tiled=True)]
    all_to_all x0 -> x1, waiting for transfers between devices: none -> 45.1 us  [shards(): columns = jnp.concatenate(lax.all_to_all(outgoing, 'req', 0, 0), axis=1)]
    all_gather x1 -> x0, waiting for transfers between devices: 31.2 us -> none  [shards(): columns = lax.all_gather(head, 'req', axis=1, tiled=True)]
    all_to_all x0 -> x1, local copies, waits for them, and re-layouts: none -> 6.46 us  [shards(): columns = jnp.concatenate(lax.all_to_all(outgoing, 'req', 0, 0), axis=1)]
    unnamed x10 -> x11, local copies, waits for them, and re-layouts: 3.44 us -> 9.75 us
    all_to_all x0 -> x1, starting transfers between devices: none -> 5 us  [shards(): columns = jnp.concatenate(lax.all_to_all(outgoing, 'req', 0, 0), axis=1)]
    another operation x0 -> x1, local copies, waits for them, and re-layouts: none -> 3.73 us  [shards(): outgoing = jnp.stack([head] * lax.axis_size('req'))]
    all_gather x3, blocking collectives: 42.2 us -> 38.6 us  [gathered_once(): both, at, found = (lax.all_gather(jnp.concatenate(lines), axis), 0, {})]
  transfers between devices with their start and end apart: 2 -> 2, of which waited for: 2 -> 2; matrix products, arithmetic and copies ran while one was open for 7% -> 9% of each run, Pallas kernels for 0% -> 0%
where the time goes in v1:
time: 217 us; the launch traced here: 216 us
  waiting for transfers between devices  83.1 us (38%)
  blocking collectives  38.6 us (18%)
  local copies, waits for them, and re-layouts  28.6 us (13%)
  matrix products  23.5 us (11%)
  other arithmetic  20.9 us (10%)
  between operations  14.2 us (7%)
  starting transfers between devices  5.04 us (2%)
  loops' own time  2.75 us (1%)
    all_to_all x1, waiting for transfers between devices, shards(): columns = jnp.concatenate(lax.all_to_all(outgoing, 'req', 0, 0), axis=1)  45.1 us
    all_gather x3, blocking collectives, gathered_once(): both, at, found = (lax.all_gather(jnp.concatenate(lines), axis), 0, {})  38.6 us
    all_gather x1, waiting for transfers between devices, shards(): full_rows = lax.all_gather(hidden, VOCAB, axis=1, tiled=True)  37.3 us
    dot_general x4, matrix products, block_logits(): return jnp.dot(rows_blk, columns, preferred_element_type=jnp.float32)  23.5 us
    unnamed x11, local copies, waits for them, and re-layouts  9.75 us
    convert_element_type x1, other arithmetic, shards(): (values * lax.rsqrt(mean_sq + EPS)[:, None] * gain[None, :]).astype(jnp.b...  8.73 us
    reduce_sum x1, other arithmetic, shards(): mean_sq = jnp.sum(values * values, axis=1) / D  7.68 us
    all_to_all x1, local copies, waits for them, and re-layouts, shards(): columns = jnp.concatenate(lax.all_to_all(outgoing, 'req', 0, 0), axis=1)  6.46 us
  transfers between devices with their start and end apart: 2, of which 2 were waited for; matrix products, arithmetic and copies ran while one was open for 9% of the time, Pallas kernels for 0%

profile of v1, /device:TPU:1, one launch (start us, length us, event | category | flops | bytes accessed | tf_op | source)
XLA Modules:
  0.0 216.5 jit_solution(2645708235544174236)
XLA Ops:
  7.2 0.7 all-gather.8.cloned.1.call-update
  7.9 3.7 %stack.2 = bf16[4,4096,128]{2,1,0:T(8,128)(2,1)} broadcast(bf16[4096,128]{1,0:T(8,128)(2,1)} %param.9), dimensions={1,2} | broadcast | bytes 5242880 | tf_op jit(solution)/shard_map/stack | solution.py:79
  11.6 5.0 %all-to-all-start = ((bf16[4,4096,128]{2,1,0:T(8,128)(2,1)}), bf16[4,4096,128]{2,1,0:T(8,128)(2,1)}, u32[]{:S(2)}, u32[]{:S(2)}) async-start(bf16[4,4096,128]{2,1,0:T(8,128)(2,1)} %stack.2), calls=%async_computation | async-start | bytes 8388608 | tf_op jit(solution)/shard_map/all_to_all | solution.py:80
  18.1 0.7 bitcast_subtract_fusion
  18.7 45.1 %all-to-all-done = bf16[4,4096,128]{2,1,0:T(8,128)(2,1)} async-done(((bf16[4,4096,128]{2,1,0:T(8,128)(2,1)}), bf16[4,4096,128]{2,1,0:T(8,128)(2,1)}, u32[]{:S(2)}, u32[]{:S(2)}) %all-to-all-start) | async-done | bytes 4194336 | tf_op jit(solution)/shard_map/all_to_all | solution.py:80
  63.8 6.5 %copy.14 = bf16[4,4096,128]{1,2,0:T(8,128)(2,1)} copy(bf16[4,4096,128]{2,1,0:T(8,128)(2,1)} %all-to-all-done) | data formatting | bytes 8388608 | tf_op jit(solution)/shard_map/all_to_all | solution.py:80
  70.2 6.6 %copy.16 = bf16[4096,512]{1,0:T(8,128)(2,1)} copy(bf16[4096,512]{0,1:T(8,128)(2,1)} %bitcast.450) | data formatting | bytes 8388608
  76.9 37.3 %all-gather.8.cloned.1.call-done = bf16[2048,4096]{0,1:T(8,128)(2,1)} async-done(((bf16[2048,64]{0,1:T(8,128)(2,1)}), bf16[2048,4096]{0,1:T(8,128)(2,1)}) %all-gather.8.cloned.1.call-update) | async-done | bytes 16777232 | tf_op jit(solution)/shard_map/all_gather | solution.py:75
  114.2 7.7 %fusion.16 = f32[2048]{0:T(1024)S(1)} fusion(bf16[2048,4096]{0,1:T(8,128)(2,1)} %all-gather.8.cloned.1.call-done), kind=kLoop, calls=%fused_computation.24 | loop fusion | flops 25163776 | bytes 16785408 | tf_op jit(solution)/shard_map/reduce_sum | solution.py:77
  121.9 3.1 %copy-done = bf16[2048,4096]{0,1:T(8,128)(2,1)S(1)} copy-done((bf16[2048,4096]{0,1:T(8,128)(2,1)S(1)}, bf16[2048,4096]{0,1:T(8,128)(2,1)}, u32[]{:S(2)}) %copy-start) | copy-done | bytes 16777240
  125.0 8.7 %fusion.18 = bf16[2048,4096]{0,1:T(8,128)(2,1)} fusion(bf16[2048,4096]{0,1:T(8,128)(2,1)S(1)} %copy-done, f32[4096]{0:T(1024)S(1)} %copy-done.1, f32[2048]{0:T(1024)S(1)} %add_rsqrt_fusion), kind=kLoop, calls=%fused_computation.26 | loop fusion | flops 33554432 | bytes 33579008 | tf_op jit(solution)/shard_map/convert_element_type | solution.py:78
  133.7 33.8 %while.17 = (s32[]{:T(128)}, f32[4,512]{1,0:T(4,128)S(1)}, f32[4,512]{1,0:T(4,128)S(1)}, f32[4,512]{1,0:T(4,128)S(1)}, f32[4,512]{1,0:T(4,128)S(1)}, /*index=5*/...) while((s32[]{:T(128)}, f32[4,512]{1,0:T(4,128)S(1)}, ...), condition=%wide.region_7.8_spmd.clone, body=%wide.region_2.7_spmd.clone.sunk | while | flops 2149586432 | bytes 10522843 | solution.py:100
  134.9 5.9 %fusion.105 = (f32[512]{0:T(512)S(1)}, f32[512,512]{0,1:T(8,128)S(1)}) fusion(bf16[4096,512]{1,0:T(8,128)(2,1)} %get-tuple-element.266, bf16[2048,4096]{0,1:T(8,128)(2,1)} %get-tuple-element.265, s32[]{:T(128)S(6)} %select_n.72), kind=kOutput, calls=%fused_computation.187.clone.1 | convolution fusion | flops 2147745280 | bytes 9439236 | tf_op jit(solution)/shard_map/while/body/eval_jaxpr/dot_general | solution.py:84
  140.8 0.8 dynamic_slice.30
  143.4 5.9 %fusion.105 = (f32[512]{0:T(512)S(1)}, f32[512,512]{0,1:T(8,128)S(1)}) fusion(bf16[4096,512]{1,0:T(8,128)(2,1)} %get-tuple-element.266, bf16[2048,4096]{0,1:T(8,128)(2,1)} %get-tuple-element.265, s32[]{:T(128)S(6)} %select_n.72), kind=kOutput, calls=%fused_computation.187.clone.1 | convolution fusion | flops 2147745280 | bytes 9439236 | tf_op jit(solution)/shard_map/while/body/eval_jaxpr/dot_general | solution.py:84
  149.3 0.8 dynamic_slice.30
  151.9 5.9 %fusion.105 = (f32[512]{0:T(512)S(1)}, f32[512,512]{0,1:T(8,128)S(1)}) fusion(bf16[4096,512]{1,0:T(8,128)(2,1)} %get-tuple-element.266, bf16[2048,4096]{0,1:T(8,128)(2,1)} %get-tuple-element.265, s32[]{:T(128)S(6)} %select_n.72), kind=kOutput, calls=%fused_computation.187.clone.1 | convolution fusion | flops 2147745280 | bytes 9439236 | tf_op jit(solution)/shard_map/while/body/eval_jaxpr/dot_general | solution.py:84
  157.7 0.8 dynamic_slice.30
  160.3 5.9 %fusion.105 = (f32[512]{0:T(512)S(1)}, f32[512,512]{0,1:T(8,128)S(1)}) fusion(bf16[4096,512]{1,0:T(8,128)(2,1)} %get-tuple-element.266, bf16[2048,4096]{0,1:T(8,128)(2,1)} %get-tuple-element.265, s32[]{:T(128)S(6)} %select_n.72), kind=kOutput, calls=%fused_computation.187.clone.1 | convolution fusion | flops 2147745280 | bytes 9439236 | tf_op jit(solution)/shard_map/while/body/eval_jaxpr/dot_general | solution.py:84
  166.2 0.8 dynamic_slice.30
  167.6 18.8 %all-gather.3 = f32[8,4,2048]{2,1,0:T(4,128)S(1)} all-gather(f32[1,4,2048]{2,1,0:T(4,128)S(1)} %maximum_bitcast_fusion), channel_id=2, replica_groups=mesh['req'=4,'vocab_0'=8,'vocab_1'=4,'vocab_2'=2] {'vocab_0'}, dimensions={0}, use_global_device_ids=true | all-gather | bytes 294912 | tf_op jit(solution)/shard_map/all_gather | solution.py:22
  186.9 9.1 %all-gather.4 = f32[4,4,2048]{2,1,0:T(4,128)S(1)} all-gather(f32[1,4,2048]{2,1,0:T(4,128)S(1)} %maximum_bitcast_fusion.1), channel_id=3, replica_groups=mesh['req'=4,'vocab_0'=8,'vocab_1'=4,'vocab_2'=2] {'vocab_1'}, dimensions={0}, use_global_device_ids=true | all-gather | bytes 163840 | tf_op jit(solution)/shard_map/all_gather | solution.py:22
  196.3 10.7 %all-gather.5 = f32[2,4,2048]{2,1,0:T(4,128)S(1)} all-gather(f32[1,4,2048]{2,1,0:T(4,128)S(1)} %maximum_bitcast_fusion.2), channel_id=4, replica_groups=mesh['req'=4,'vocab_0'=8,'vocab_1'=4,'vocab_2'=2] {'vocab_2'}, dimensions={0}, use_global_device_ids=true | all-gather | bytes 98304 | tf_op jit(solution)/shard_map/all_gather | solution.py:22
  207.0 0.7 subtract_select_fusion
  (61 shorter events, 8.8 us)
Async XLA Ops:
  7.2 107.0 %all-gather.8.cloned.1.call-start = ((), (), s32[]{:S(2)}) async-start(), calls=%async_computation.1 | async-start | bytes 17039360 | tf_op jit(solution)/shard_map/all_gather | solution.py:75
  11.6 52.1 %all-to-all-start = ((bf16[4,4096,128]{2,1,0:T(8,128)(2,1)}), bf16[4,4096,128]{2,1,0:T(8,128)(2,1)}, u32[]{:S(2)}, u32[]{:S(2)}) async-start(bf16[4,4096,128]{2,1,0:T(8,128)(2,1)} %stack.2), calls=%async_computation | async-start | bytes 8388608 | tf_op jit(solution)/shard_map/all_to_all | solution.py:80
  18.7 103.2 %copy-start.1 = (f32[4096]{0:T(1024)S(1)}, f32[4096]{0:T(1024)}, u32[]{:S(2)}) copy-start(f32[4096]{0:T(1024)} %param.8) | copy-start | bytes 49156
  114.2 10.8 %copy-start = (bf16[2048,4096]{0,1:T(8,128)(2,1)S(1)}, bf16[2048,4096]{0,1:T(8,128)(2,1)}, u32[]{:S(2)}) copy-start(bf16[2048,4096]{0,1:T(8,128)(2,1)} %all-gather.8.cloned.1.call-done) | copy-start | bytes 50331652
  133.7 75.4 %copy-start.2 = (s32[1,4]{1,0:T(1,128)S(1)}, s32[1,4]{1,0:T(1,128)}, u32[]{:S(2)}) copy-start(s32[1,4]{1,0:T(1,128)} %param.11) | copy-start | bytes 52
Sparse Core Ops, SparseCore 0:
  10.7 103.3 all-gather.7
